TPU v7x, 128 devices: a whole 4x4x4 slice. The times are simulated.
128 devices in a mesh: expert: 8 (over x, core), cuts: 16 (over y, z).
Axes of the slice: x: 4, y: 4, z: 4, core: 2. Of those that a mesh axis runs over, the one named last changes fastest.
Arguments:
- tokens: bfloat16 [1024, 4096], P('expert', 'cuts'), may hold values from -6 to 6
- routing: int32 [1024, 2], P('expert'), may hold values from 0 to 7, all different within a row; in each aligned block of 128 rows (0 to 127, 128 to 255, ...) at most 64 rows name the same one
- gates: float32 [1024, 2], P('expert'), may hold values from 0.2 to 1
- cotangent: bfloat16 [1024, 4096], P('expert', 'cuts'), may hold values from -6 to 6
- w_gate: bfloat16 [8, 4096, 8192], P('expert', None, 'cuts'), may hold values from -0.09375 to 0.09375
- w_up: bfloat16 [8, 4096, 8192], P('expert', None, 'cuts'), may hold values from -0.09375 to 0.09375
- w_down: bfloat16 [8, 8192, 4096], P('expert', 'cuts'), may hold values from -0.0625 to 0.0625
Outputs:
- mixed: bfloat16 [1024, 4096], P('expert', 'cuts')
- grad_tokens: bfloat16 [1024, 4096], P('expert', 'cuts')
- grad_gates: float32 [1024, 2], P('expert')
- grad_w_gate: bfloat16 [8, 4096, 8192], P('expert', None, 'cuts')
- grad_w_up: bfloat16 [8, 4096, 8192], P('expert', None, 'cuts')
- grad_w_down: bfloat16 [8, 8192, 4096], P('expert', 'cuts')
Inputs may be any that keep to these rules, and one draw needn't show every extreme that they name: `routing`: in each aligned block of 128 rows (the tokens owned by one position along `expert`) no expert is named by more than 64 rows, a bound that some block reaches.
All inputs are finite; a program needn't handle non-finite values.
Results may differ from a plain program's by a relative error of at most 0.015.
Values may be sent and summed in bfloat16 or wider, within the bound.
A program may use at most 128 MiB of HBM per device.

v0:
```python
import jax
import jax.numpy as jnp
from jax import lax
from jax.sharding import PartitionSpec as P


def slot_tables(routing, experts, capacity):
    row_count = routing.shape[0]
    flat_route = routing.reshape(-1)
    onehot = (flat_route[:, None] == jnp.arange(experts, dtype=jnp.int32)[None, :]).astype(
        jnp.int32
    )
    before = jnp.cumsum(onehot, axis=0) - onehot
    position = jnp.sum(before * onehot, axis=1)
    destination = (flat_route * capacity + position).reshape(row_count, 2)
    slot_ids = jnp.arange(experts * capacity, dtype=jnp.int32)
    pick_first = (slot_ids[:, None] == destination[None, :, 0]).astype(jnp.bfloat16)
    pick_second = (slot_ids[:, None] == destination[None, :, 1]).astype(jnp.bfloat16)
    return (destination, pick_first, pick_second)


def local(tokens, routing, gates, cotangent, w_gate, w_up, w_down):
    experts = lax.axis_size("expert")
    capacity = tokens.shape[0] // 2
    destination, pick_first, pick_second = slot_tables(routing, experts, capacity)
    x_send = jnp.dot(pick_first + pick_second, tokens, preferred_element_type=jnp.float32).astype(
        jnp.bfloat16
    )
    grad_out = cotangent.astype(jnp.float32)
    grad_first = (gates[:, 0:1] * grad_out).astype(jnp.bfloat16)
    grad_second = (gates[:, 1:2] * grad_out).astype(jnp.bfloat16)
    d_send = (
        jnp.dot(pick_first, grad_first, preferred_element_type=jnp.float32)
        + jnp.dot(pick_second, grad_second, preferred_element_type=jnp.float32)
    ).astype(jnp.bfloat16)
    x_recv, d_recv = (
        lax.all_to_all(x_send, "expert", split_axis=0, concat_axis=0, tiled=True),
        lax.all_to_all(d_send, "expert", split_axis=0, concat_axis=0, tiled=True),
    )
    x_rows, d_rows = (
        lax.all_gather(x_recv, "cuts", axis=1, tiled=True),
        lax.all_gather(d_recv, "cuts", axis=1, tiled=True),
    )

    def send_home(partial_value):
        owned_sum = lax.psum_scatter(
            partial_value.astype(jnp.bfloat16), "cuts", scatter_dimension=1, tiled=True
        )
        return lax.all_to_all(owned_sum, "expert", split_axis=0, concat_axis=0, tiled=True)

    gate_w = w_gate[0]
    up_w = w_up[0]
    down_w = w_down[0]
    gate_pre = jnp.dot(x_rows, gate_w, preferred_element_type=jnp.float32)
    up_pre = jnp.dot(x_rows, up_w, preferred_element_type=jnp.float32)
    sigmoid_gate = jax.nn.sigmoid(gate_pre)
    activated = gate_pre * sigmoid_gate
    hidden = (activated * up_pre).astype(jnp.bfloat16)
    out_partial = jnp.dot(hidden, down_w, preferred_element_type=jnp.float32)
    out_home = send_home(out_partial)
    out_first = out_home[destination[:, 0]].astype(jnp.float32)
    out_second = out_home[destination[:, 1]].astype(jnp.float32)
    mixed = (gates[:, 0:1] * out_first + gates[:, 1:2] * out_second).astype(jnp.bfloat16)
    dot_terms = jnp.stack(
        [jnp.sum(grad_out * out_first, axis=1), jnp.sum(grad_out * out_second, axis=1)], axis=1
    )
    grad_gates = lax.psum(dot_terms, "cuts")
    grad_hidden = lax.dot_general(
        d_rows, down_w, (((1,), (1,)), ((), ())), preferred_element_type=jnp.float32
    )
    grad_gate_pre = (
        grad_hidden * up_pre * sigmoid_gate * (1.0 + gate_pre * (1.0 - sigmoid_gate))
    ).astype(jnp.bfloat16)
    grad_up_pre = (grad_hidden * activated).astype(jnp.bfloat16)
    grad_down = lax.dot_general(
        hidden, d_rows, (((0,), (0,)), ((), ())), preferred_element_type=jnp.float32
    ).astype(jnp.bfloat16)
    grad_gate_w = lax.dot_general(
        x_rows, grad_gate_pre, (((0,), (0,)), ((), ())), preferred_element_type=jnp.float32
    ).astype(jnp.bfloat16)
    grad_up_w = lax.dot_general(
        x_rows, grad_up_pre, (((0,), (0,)), ((), ())), preferred_element_type=jnp.float32
    ).astype(jnp.bfloat16)
    row_partial = lax.dot_general(
        grad_gate_pre, gate_w, (((1,), (1,)), ((), ())), preferred_element_type=jnp.float32
    )
    row_partial = row_partial + lax.dot_general(
        grad_up_pre, up_w, (((1,), (1,)), ((), ())), preferred_element_type=jnp.float32
    )
    grad_home = send_home(row_partial)
    grad_tokens = (
        gates[:, 0:1] * grad_home[destination[:, 0]].astype(jnp.float32)
        + gates[:, 1:2] * grad_home[destination[:, 1]].astype(jnp.float32)
    ).astype(jnp.bfloat16)
    return (mixed, grad_tokens, grad_gates, grad_gate_w[None], grad_up_w[None], grad_down[None])


def solution(mesh):
    return jax.shard_map(
        local,
        mesh=mesh,
        in_specs=(
            P("expert", "cuts"),
            P("expert", None),
            P("expert", None),
            P("expert", "cuts"),
            P("expert", None, "cuts"),
            P("expert", None, "cuts"),
            P("expert", "cuts", None),
        ),
        out_specs=(
            P("expert", "cuts"),
            P("expert", "cuts"),
            P("expert", None),
            P("expert", None, "cuts"),
            P("expert", None, "cuts"),
            P("expert", "cuts", None),
        ),
        check_vma=False,
    )
```

profile of v0, /device:TPU:2, one launch (start us, length us, event | category | flops | bytes accessed | tf_op | source)
XLA Modules:
  0.0 372.2 jit_solution(16859567116568932094)
XLA Ops:
  7.2 0.0 copy-start
  7.2 0.0 all-gather.3.cloned.1.call-start
  7.2 0.8 copy.21
  8.0 0.1 eq.60
  8.2 0.1 eq.56
  8.3 0.6 reduce-window.6
  8.9 0.2 slice_reduce_fusion
  9.2 0.1 fusion.36
  9.2 0.1 reduce_sum.30
  9.4 0.1 copy.23
  9.5 0.7 multiply_add_fusion
  10.2 0.2 convolution_convert_fusion.4
  10.4 10.8 %all_to_all.48 = bf16[8,64,256]{2,1,0:T(8,128)(2,1)} all-to-all(bf16[8,64,256]{2,1,0:T(8,128)(2,1)S(1)} %bitcast.70), channel_id=1, replica_groups=mesh['expert'=8,'cuts'=16] {'expert'}, dimensions={0} | all-to-all | bytes 524288 | tf_op jit(solution)/shard_map/all_to_all | solution.py:37
  21.2 0.0 all-gather.3.cloned.1.call-update
  21.2 0.0 all-gather.5.cloned.1.call-start
  21.2 0.8 slice_bitcast_fusion.1
  22.0 1.1 fusion.16
  23.1 1.1 fusion.13
  24.3 10.6 %all_to_all.49 = bf16[8,64,256]{2,1,0:T(8,128)(2,1)} all-to-all(bf16[8,64,256]{2,1,0:T(8,128)(2,1)S(1)} %bitcast.73), channel_id=1, replica_groups=mesh['expert'=8,'cuts'=16] {'expert'}, dimensions={0} | all-to-all | bytes 524288 | tf_op jit(solution)/shard_map/all_to_all | solution.py:38
  34.9 0.0 all-gather.5.cloned.1.call-update
  34.9 0.0 reduce-scatter.5.cloned.1.call-start
  34.9 44.8 %all-gather.3.cloned.1.call-done = bf16[512,4096]{1,0:T(8,128)(2,1)} async-done(((bf16[512,256]{1,0:T(8,128)(2,1)}), bf16[512,4096]{1,0:T(8,128)(2,1)}) %all-gather.3.cloned.1.call-update) | async-done | bytes 4194320 | tf_op jit(solution)/shard_map/all_gather | solution.py:41
  79.8 5.9 %fusion.11 = f32[512,512]{1,0:T(8,128)S(1)} fusion(bf16[512,4096]{1,0:T(8,128)(2,1)} %all-gather.3.cloned.1.call-done, bf16[1,4096,512]{2,1,0:T(8,128)(2,1)} %param.11), kind=kOutput, calls=%fused_computation.20 | convolution fusion | flops 2147483648 | bytes 9437184 | tf_op jit(solution)/shard_map/dot_general | solution.py:54
  85.7 3.3 fusion.7
  89.0 49.1 %all-gather.5.cloned.1.call-done = bf16[512,4096]{1,0:T(8,128)(2,1)} async-done(((bf16[512,256]{1,0:T(8,128)(2,1)}), bf16[512,4096]{1,0:T(8,128)(2,1)}) %all-gather.5.cloned.1.call-update) | async-done | bytes 4194320 | tf_op jit(solution)/shard_map/all_gather | solution.py:42
  138.1 6.6 %multiply_convert_fusion = (bf16[512,512]{1,0:T(8,128)(2,1)S(1)}, bf16[512,512]{1,0:T(8,128)(2,1)S(1)}, bf16[512,512]{1,0:T(8,128)(2,1)S(1)}) fusion(f32[512,512]{1,0:T(8,128)S(1)} %fusion.11, f32[512,512]{1,0:T(8,128)} %fusion.7, bf16[512,4096]{1,0:T(8,128)(2,1)} %all-gather.5.cloned.1.call-done, bf16[1,512,4096]{2,1,0:T(8,128)(2,1)} %param.13), kind=kOutput, calls=%fused_computation.25 | convolution fusion | flops 2151415808 | bytes 12058624 | tf_op jit(solution)/shard_map/dot_general | solution.py:68
  144.7 0.0 copy-start.3
  144.7 2.4 fusion.9
  147.2 4.5 %add_convert_fusion = bf16[512,4096]{1,0:T(8,128)(2,1)} fusion(f32[512,4096]{1,0:T(8,128)S(1)} %fusion.9, bf16[512,512]{1,0:T(8,128)(2,1)S(1)} %get-tuple-element.8, bf16[1,4096,512]{2,1,0:T(8,128)(2,1)S(1)} %copy-done.3), kind=kOutput, calls=%fused_computation.4 | convolution fusion | flops 2151677952 | bytes 17301504 | tf_op jit(solution)/shard_map/dot_general | solution.py:87
  151.7 0.0 reduce-scatter.5.cloned.1.call-update
  151.7 0.2 reduce-scatter.3.cloned.1.call-start
  151.9 6.6 %convolution_convert_fusion.3 = bf16[512,4096]{1,0:T(8,128)(2,1)} fusion(bf16[512,512]{1,0:T(8,128)(2,1)S(1)} %get-tuple-element.10, bf16[1,512,4096]{2,1,0:T(8,128)(2,1)} %param.13), kind=kOutput, calls=%fused_computation.8 | convolution fusion | flops 2149580800 | bytes 8912896 | tf_op jit(solution)/shard_map/dot_general | solution.py:59
  158.5 0.0 reduce-scatter.3.cloned.1.call-update
  158.5 6.7 %fusion.2 = bf16[1,512,4096]{2,1,0:T(8,128)(2,1)} fusion(bf16[512,512]{1,0:T(8,128)(2,1)S(1)} %get-tuple-element.10, bf16[512,4096]{1,0:T(8,128)(2,1)} %all-gather.5.cloned.1.call-done), kind=kOutput, calls=%fused_computation.11 | convolution fusion | flops 2149580800 | bytes 8912896 | tf_op jit(solution)/shard_map/dot_general | solution.py:75
  165.2 64.6 %reduce-scatter.5.cloned.1.call-done = bf16[512,256]{1,0:T(8,128)(2,1)} async-done(((bf16[512,4096]{1,0:T(8,128)(2,1)}), bf16[512,256]{1,0:T(8,128)(2,1)}) %reduce-scatter.5.cloned.1.call-update) | async-done | bytes 262160 | tf_op jit(solution)/shard_map/reduce_scatter | solution.py:46
  229.8 4.8 %all-to-all-start.3 = ((bf16[8,64,256]{2,1,0:T(8,128)(2,1)}), bf16[8,64,256]{2,1,0:T(8,128)(2,1)S(1)}, u32[]{:S(2)}, u32[]{:S(2)}) async-start(bf16[8,64,256]{2,1,0:T(8,128)(2,1)} %bitcast.75), calls=%async_computation.5 | async-start | bytes 524288 | tf_op jit(solution)/shard_map/all_to_all | solution.py:49
  234.6 6.6 %fusion = bf16[1,4096,512]{2,1,0:T(8,128)(2,1)} fusion(bf16[512,4096]{1,0:T(8,128)(2,1)} %all-gather.3.cloned.1.call-done, bf16[512,512]{1,0:T(8,128)(2,1)S(1)} %get-tuple-element.9), kind=kOutput, calls=%fused_computation.9 | convolution fusion | flops 2149580800 | bytes 8912896 | tf_op jit(solution)/shard_map/dot_general | solution.py:78
  241.2 70.1 %reduce-scatter.3.cloned.1.call-done = bf16[512,256]{1,0:T(8,128)(2,1)} async-done(((bf16[512,4096]{1,0:T(8,128)(2,1)}), bf16[512,256]{1,0:T(8,128)(2,1)}) %reduce-scatter.3.cloned.1.call-update) | async-done | bytes 262160 | tf_op jit(solution)/shard_map/reduce_scatter | solution.py:46
  311.2 0.0 all-to-all-done.3
  311.2 4.8 %all-to-all-start.1 = ((bf16[8,64,256]{2,1,0:T(8,128)(2,1)}), bf16[8,64,256]{2,1,0:T(8,128)(2,1)S(1)}, u32[]{:S(2)}, u32[]{:S(2)}) async-start(bf16[8,64,256]{2,1,0:T(8,128)(2,1)} %bitcast.74), calls=%async_computation.2 | async-start | bytes 524288 | tf_op jit(solution)/shard_map/all_to_all | solution.py:49
  316.1 6.6 %fusion.1 = bf16[1,4096,512]{2,1,0:T(8,128)(2,1)} fusion(bf16[512,4096]{1,0:T(8,128)(2,1)} %all-gather.3.cloned.1.call-done, bf16[512,512]{1,0:T(8,128)(2,1)S(1)} %get-tuple-element.8), kind=kOutput, calls=%fused_computation.10 | convolution fusion | flops 2149580800 | bytes 8912896 | tf_op jit(solution)/shard_map/dot_general | solution.py:81
  322.7 0.8 gather_fusion.2
  323.5 0.8 gather_fusion.3
  324.4 0.0 all-to-all-done.1
  324.4 0.8 gather_fusion.1
  325.2 0.8 gather_fusion
  326.1 0.8 fusion.22
  326.9 38.7 %psum.7 = f32[128,2]{0,1:T(2,128)} all-reduce(f32[128,2]{0,1:T(2,128)S(1)} %pad_maximum_fusion), channel_id=1, replica_groups=mesh['expert'=8,'cuts'=16] {'cuts'}, use_global_device_ids=true, to_apply=%region_7.8 | all-reduce | flops 256 | bytes 2048 | tf_op jit(solution)/shard_map/psum | solution.py:67
  (16 shorter events, 0.1 us)
Async XLA Ops:
  7.2 3.0 copy-start
  7.2 72.6 %all-gather.3.cloned.1.call-start = ((), (), s32[]{:S(2)}) async-start(), calls=%async_computation.6 | async-start | bytes 4456448 | tf_op jit(solution)/shard_map/all_gather | solution.py:41
  21.2 116.9 %all-gather.5.cloned.1.call-start = ((), (), s32[]{:S(2)}) async-start(), calls=%async_computation.8 | async-start | bytes 4456448 | tf_op jit(solution)/shard_map/all_gather | solution.py:42
  34.9 194.9 %reduce-scatter.5.cloned.1.call-start = ((), (), s32[]{:S(2)}) async-start(), calls=%async_computation.9 | async-start | bytes 4456448 | tf_op jit(solution)/shard_map/reduce_scatter | solution.py:46
  79.8 5.9 %copy-start.2 = (bf16[1,4096,512]{2,1,0:T(8,128)(2,1)S(1)}, bf16[1,4096,512]{2,1,0:T(8,128)(2,1)}, u32[]{:S(2)}) copy-start(bf16[1,4096,512]{2,1,0:T(8,128)(2,1)} %param.12) | copy-start | bytes 12582916
  79.8 5.9 %copy-start.5 = (bf16[512,4096]{1,0:T(8,128)(2,1)S(1)}, bf16[512,4096]{1,0:T(8,128)(2,1)}, u32[]{:S(2)}) copy-start(bf16[512,4096]{1,0:T(8,128)(2,1)} %all-gather.3.cloned.1.call-done) | copy-start | bytes 12582916
  138.1 6.6 %copy-start.1 = (bf16[1,4096,512]{2,1,0:T(8,128)(2,1)S(1)}, bf16[1,4096,512]{2,1,0:T(8,128)(2,1)}, u32[]{:S(2)}) copy-start(bf16[1,4096,512]{2,1,0:T(8,128)(2,1)} %param.11) | copy-start | bytes 12582916
  144.7 2.4 copy-start.3
  151.7 159.5 %reduce-scatter.3.cloned.1.call-start = ((), (), s32[]{:S(2)}) async-start(), calls=%async_computation.7 | async-start | bytes 4456448 | tf_op jit(solution)/shard_map/reduce_scatter | solution.py:46
  229.8 81.5 %all-to-all-start.3 = ((bf16[8,64,256]{2,1,0:T(8,128)(2,1)}), bf16[8,64,256]{2,1,0:T(8,128)(2,1)S(1)}, u32[]{:S(2)}, u32[]{:S(2)}) async-start(bf16[8,64,256]{2,1,0:T(8,128)(2,1)} %bitcast.75), calls=%async_computation.5 | async-start | bytes 524288 | tf_op jit(solution)/shard_map/all_to_all | solution.py:49
  311.2 13.1 %all-to-all-start.1 = ((bf16[8,64,256]{2,1,0:T(8,128)(2,1)}), bf16[8,64,256]{2,1,0:T(8,128)(2,1)S(1)}, u32[]{:S(2)}, u32[]{:S(2)}) async-start(bf16[8,64,256]{2,1,0:T(8,128)(2,1)} %bitcast.74), calls=%async_computation.2 | async-start | bytes 524288 | tf_op jit(solution)/shard_map/all_to_all | solution.py:49
  316.1 10.0 %copy-start.4 = (bf16[128,256]{1,0:T(8,128)(2,1)S(1)}, bf16[128,256]{1,0:T(8,128)(2,1)}, u32[]{:S(2)}) copy-start(bf16[128,256]{1,0:T(8,128)(2,1)} %param.10) | copy-start | bytes 196612
Sparse Core Ops, SparseCore 0:
  21.3 58.3 all-gather.2
  81.9 56.2 all-gather.4
  151.8 77.9 reduce-scatter.4
  233.5 77.6 reduce-scatter.2
where the time goes:
time: 373 us; the launch traced here: 372 us
  waiting for transfers between devices  229 us (61%)
  blocking collectives  60.1 us (16%)
  matrix products  51.6 us (14%)
  between operations  13.9 us (4%)
  starting transfers between devices  9.97 us (3%)
  local copies, waits for them, and re-layouts  5.66 us (2%)
    reduce_scatter x2, waiting for transfers between devices, send_home(): lax.psum_scatter(partial_value.astype(jnp.bfloat16), 'cuts', scatter_dime...  135 us
    all_gather x1, waiting for transfers between devices, local(): lax.all_gather(d_recv, 'cuts', axis=1, tiled=True)  49.1 us
    all_gather x1, waiting for transfers between devices, local(): lax.all_gather(x_recv, 'cuts', axis=1, tiled=True)  44.8 us
    psum x1, blocking collectives, local(): grad_gates = lax.psum(dot_terms, 'cuts')  38.7 us
    all_to_all x1, blocking collectives, local(): lax.all_to_all(x_send, 'expert', split_axis=0, concat_axis=0, tiled=True)  10.8 us
    all_to_all x1, blocking collectives, local(): lax.all_to_all(d_send, 'expert', split_axis=0, concat_axis=0, tiled=True)  10.6 us
    all_to_all x2, starting transfers between devices, send_home(): lax.all_to_all(owned_sum, 'expert', split_axis=0, concat_axis=0, tiled=True)  9.62 us
  transfers between devices with their start and end apart: 6, of which 4 were waited for; matrix products, arithmetic and copies ran while one was open for 11% of the time, Pallas kernels for 0%

commit v1 on v0

--- a/solution.py
+++ b/solution.py
@@ -64,7 +64,11 @@
     dot_terms = jnp.stack(
         [jnp.sum(grad_out * out_first, axis=1), jnp.sum(grad_out * out_second, axis=1)], axis=1
     )
-    grad_gates = lax.psum(dot_terms, "cuts")
+    grad_gates = dot_terms
+    for hop in (1, 2, 4, 8):
+        grad_gates = grad_gates + lax.ppermute(
+            grad_gates, "cuts", [(dev, dev ^ hop) for dev in range(16)]
+        )
     grad_hidden = lax.dot_general(
         d_rows, down_w, (((1,), (1,)), ((), ())), preferred_element_type=jnp.float32
     )

time: 373 us -> 358 us (0.960)
  blocking collectives: 60.1 us -> 21.4 us
  waiting for transfers between devices: 229 us -> 249 us
  starting transfers between devices: 9.97 us -> 16.6 us
  matrix products: 51.6 us -> 47.3 us
    psum x1 -> x0, blocking collectives: 38.7 us -> none  [local(): grad_gates = lax.psum(dot_terms, 'cuts')]
    reduce_scatter x2, waiting for transfers between devices: 135 us -> 148 us  [send_home(): lax.psum_scatter(partial_value.astype(jnp.bfloat16), 'cuts', scatter_dime...]
    ppermute x0 -> x4, starting transfers between devices: none -> 6.67 us  [local(): lax.ppermute(grad_gates, 'cuts', [(dev, dev ^ hop) for dev in range(16)])]
    all_to_all x2, waiting for transfers between devices: 0.01 us -> 4.34 us  [send_home(): lax.all_to_all(owned_sum, 'expert', split_axis=0, concat_axis=0, tiled=True)]
  transfers between devices with their start and end apart: 6 -> 10, of which waited for: 4 -> 6; matrix products, arithmetic and copies ran while one was open for 11% -> 10% of each run, Pallas kernels for 0% -> 0%
where the time goes in v1:
time: 358 us; the launch traced here: 356 us
  waiting for transfers between devices  249 us (70%)
  matrix products  47.3 us (13%)
  blocking collectives  21.4 us (6%)
  starting transfers between devices  16.6 us (5%)
  between operations  13.9 us (4%)
  local copies, waits for them, and re-layouts  5.66 us (2%)
    reduce_scatter x2, waiting for transfers between devices, send_home(): lax.psum_scatter(partial_value.astype(jnp.bfloat16), 'cuts', scatter_dime...  148 us
    all_gather x1, waiting for transfers between devices, local(): lax.all_gather(d_recv, 'cuts', axis=1, tiled=True)  49.1 us
    all_gather x1, waiting for transfers between devices, local(): lax.all_gather(x_recv, 'cuts', axis=1, tiled=True)  44.8 us
    all_to_all x1, blocking collectives, local(): lax.all_to_all(x_send, 'expert', split_axis=0, concat_axis=0, tiled=True)  10.8 us
    all_to_all x1, blocking collectives, local(): lax.all_to_all(d_send, 'expert', split_axis=0, concat_axis=0, tiled=True)  10.6 us
    all_to_all x2, starting transfers between devices, send_home(): lax.all_to_all(owned_sum, 'expert', split_axis=0, concat_axis=0, tiled=True)  9.61 us
  transfers between devices with their start and end apart: 10, of which 6 were waited for; matrix products, arithmetic and copies ran while one was open for 10% of the time, Pallas kernels for 0%

profile of v1, /device:TPU:2, one launch (start us, length us, event | category | flops | bytes accessed | tf_op | source)
XLA Modules:
  0.0 356.5 jit_solution(3538879725584372070)
XLA Ops:
  7.2 0.0 all-gather.3.cloned.1.call-start
  7.2 0.8 copy.21
  8.0 0.1 eq.60
  8.2 0.1 eq.56
  8.3 0.6 reduce-window.6
  8.9 0.2 slice_reduce_fusion
  9.2 0.1 fusion.36
  9.2 0.1 reduce_sum.30
  9.4 0.1 copy.23
  9.5 0.7 multiply_add_fusion
  10.2 0.2 convolution_convert_fusion.4
  10.4 10.8 %all_to_all.48 = bf16[8,64,256]{2,1,0:T(8,128)(2,1)} all-to-all(bf16[8,64,256]{2,1,0:T(8,128)(2,1)S(1)} %bitcast.70), channel_id=1, replica_groups=mesh['expert'=8,'cuts'=16] {'expert'}, dimensions={0} | all-to-all | bytes 524288 | tf_op jit(solution)/shard_map/all_to_all | solution.py:37
  21.2 0.0 all-gather.3.cloned.1.call-update
  21.2 0.0 all-gather.5.cloned.1.call-start
  21.2 0.8 slice_bitcast_fusion.1
  22.0 1.1 fusion.16
  23.1 1.1 fusion.13
  24.3 10.6 %all_to_all.49 = bf16[8,64,256]{2,1,0:T(8,128)(2,1)} all-to-all(bf16[8,64,256]{2,1,0:T(8,128)(2,1)S(1)} %bitcast.73), channel_id=1, replica_groups=mesh['expert'=8,'cuts'=16] {'expert'}, dimensions={0} | all-to-all | bytes 524288 | tf_op jit(solution)/shard_map/all_to_all | solution.py:38
  34.9 0.0 all-gather.5.cloned.1.call-update
  34.9 0.0 reduce-scatter.5.cloned.1.call-start
  34.9 44.8 %all-gather.3.cloned.1.call-done = bf16[512,4096]{1,0:T(8,128)(2,1)} async-done(((bf16[512,256]{1,0:T(8,128)(2,1)}), bf16[512,4096]{1,0:T(8,128)(2,1)}) %all-gather.3.cloned.1.call-update) | async-done | bytes 4194320 | tf_op jit(solution)/shard_map/all_gather | solution.py:41
  79.8 5.9 %fusion.11 = f32[512,512]{1,0:T(8,128)S(1)} fusion(bf16[512,4096]{1,0:T(8,128)(2,1)} %all-gather.3.cloned.1.call-done, bf16[1,4096,512]{2,1,0:T(8,128)(2,1)} %param.11), kind=kOutput, calls=%fused_computation.20 | convolution fusion | flops 2147483648 | bytes 9437184 | tf_op jit(solution)/shard_map/dot_general | solution.py:54
  85.7 3.3 fusion.7
  89.0 49.1 %all-gather.5.cloned.1.call-done = bf16[512,4096]{1,0:T(8,128)(2,1)} async-done(((bf16[512,256]{1,0:T(8,128)(2,1)}), bf16[512,4096]{1,0:T(8,128)(2,1)}) %all-gather.5.cloned.1.call-update) | async-done | bytes 4194320 | tf_op jit(solution)/shard_map/all_gather | solution.py:42
  138.1 6.5 %multiply_convert_fusion = (bf16[512,512]{1,0:T(8,128)(2,1)S(1)}, bf16[512,512]{1,0:T(8,128)(2,1)S(1)}, bf16[512,512]{1,0:T(8,128)(2,1)S(1)}) fusion(f32[512,512]{1,0:T(8,128)S(1)} %fusion.11, f32[512,512]{1,0:T(8,128)} %fusion.7, bf16[512,4096]{1,0:T(8,128)(2,1)} %all-gather.5.cloned.1.call-done, bf16[1,512,4096]{2,1,0:T(8,128)(2,1)} %param.13), kind=kOutput, calls=%fused_computation.25 | convolution fusion | flops 2151415808 | bytes 12058624 | tf_op jit(solution)/shard_map/dot_general | solution.py:72
  144.7 2.4 fusion.9
  147.1 4.5 %add_convert_fusion = bf16[512,4096]{1,0:T(8,128)(2,1)} fusion(f32[512,4096]{1,0:T(8,128)S(1)} %fusion.9, bf16[512,512]{1,0:T(8,128)(2,1)S(1)} %get-tuple-element.8, bf16[1,4096,512]{2,1,0:T(8,128)(2,1)S(1)} %copy-done.3), kind=kOutput, calls=%fused_computation.4 | convolution fusion | flops 2151677952 | bytes 17301504 | tf_op jit(solution)/shard_map/dot_general | solution.py:91
  151.7 0.2 reduce-scatter.3.cloned.1.call-start
  151.9 6.6 %convolution_convert_fusion.3 = bf16[512,4096]{1,0:T(8,128)(2,1)} fusion(bf16[512,512]{1,0:T(8,128)(2,1)S(1)} %get-tuple-element.10, bf16[1,512,4096]{2,1,0:T(8,128)(2,1)} %param.13), kind=kOutput, calls=%fused_computation.8 | convolution fusion | flops 2149580800 | bytes 8912896 | tf_op jit(solution)/shard_map/dot_general | solution.py:59
  158.5 71.2 %reduce-scatter.5.cloned.1.call-done = bf16[512,256]{1,0:T(8,128)(2,1)} async-done(((bf16[512,4096]{1,0:T(8,128)(2,1)}), bf16[512,256]{1,0:T(8,128)(2,1)}) %reduce-scatter.5.cloned.1.call-update) | async-done | bytes 262160 | tf_op jit(solution)/shard_map/reduce_scatter | solution.py:46
  229.7 4.8 %all-to-all-start.3 = ((bf16[8,64,256]{2,1,0:T(8,128)(2,1)}), bf16[8,64,256]{2,1,0:T(8,128)(2,1)S(1)}, u32[]{:S(2)}, u32[]{:S(2)}) async-start(bf16[8,64,256]{2,1,0:T(8,128)(2,1)} %bitcast.75), calls=%async_computation.5 | async-start | bytes 524288 | tf_op jit(solution)/shard_map/all_to_all | solution.py:49
  234.5 76.7 %reduce-scatter.3.cloned.1.call-done = bf16[512,256]{1,0:T(8,128)(2,1)} async-done(((bf16[512,4096]{1,0:T(8,128)(2,1)}), bf16[512,256]{1,0:T(8,128)(2,1)}) %reduce-scatter.3.cloned.1.call-update) | async-done | bytes 262160 | tf_op jit(solution)/shard_map/reduce_scatter | solution.py:46
  311.2 4.8 %all-to-all-start.1 = ((bf16[8,64,256]{2,1,0:T(8,128)(2,1)}), bf16[8,64,256]{2,1,0:T(8,128)(2,1)S(1)}, u32[]{:S(2)}, u32[]{:S(2)}) async-start(bf16[8,64,256]{2,1,0:T(8,128)(2,1)} %bitcast.74), calls=%async_computation.2 | async-start | bytes 524288 | tf_op jit(solution)/shard_map/all_to_all | solution.py:49
  316.0 0.8 gather_fusion.2
  316.9 0.8 gather_fusion.3
  317.7 4.3 %all-to-all-done.1 = bf16[8,64,256]{2,1,0:T(8,128)(2,1)S(1)} async-done(((bf16[8,64,256]{2,1,0:T(8,128)(2,1)}), bf16[8,64,256]{2,1,0:T(8,128)(2,1)S(1)}, u32[]{:S(2)}, u32[]{:S(2)}) %all-to-all-start.1) | async-done | bytes 262176 | tf_op jit(solution)/shard_map/all_to_all | solution.py:49
  322.1 0.8 gather_fusion.1
  322.9 0.8 gather_fusion
  323.8 0.8 fusion.22
  324.6 1.2 collective-permute-start
  325.8 2.5 collective-permute-done
  328.3 2.6 collective-permute-start.1
  330.9 6.6 %fusion.2 = bf16[1,512,4096]{2,1,0:T(8,128)(2,1)} fusion(bf16[512,512]{1,0:T(8,128)(2,1)S(1)} %get-tuple-element.10, bf16[512,4096]{1,0:T(8,128)(2,1)} %all-gather.5.cloned.1.call-done), kind=kOutput, calls=%fused_computation.11 | convolution fusion | flops 2149580800 | bytes 8912896 | tf_op jit(solution)/shard_map/dot_general | solution.py:79
  337.4 0.3 collective-permute-start.2
  337.7 4.5 %fusion = bf16[1,4096,512]{2,1,0:T(8,128)(2,1)} fusion(bf16[512,4096]{1,0:T(8,128)(2,1)S(1)} %copy-done.6, bf16[512,512]{1,0:T(8,128)(2,1)S(1)} %get-tuple-element.9), kind=kOutput, calls=%fused_computation.9 | convolution fusion | flops 2149580800 | bytes 8912896 | tf_op jit(solution)/shard_map/dot_general | solution.py:82
  342.2 2.7 collective-permute-start.3
  344.9 4.5 %fusion.1 = bf16[1,4096,512]{2,1,0:T(8,128)(2,1)} fusion(bf16[512,4096]{1,0:T(8,128)(2,1)S(1)} %copy-done.6, bf16[512,512]{1,0:T(8,128)(2,1)S(1)} %get-tuple-element.8), kind=kOutput, calls=%fused_computation.10 | convolution fusion | flops 2149580800 | bytes 8912896 | tf_op jit(solution)/shard_map/dot_general | solution.py:85
  349.4 0.6 add.64
  (29 shorter events, 0.2 us)
Async XLA Ops:
  7.2 3.0 copy-start
  7.2 72.6 %all-gather.3.cloned.1.call-start = ((), (), s32[]{:S(2)}) async-start(), calls=%async_computation.6 | async-start | bytes 4456448 | tf_op jit(solution)/shard_map/all_gather | solution.py:41
  21.2 116.9 %all-gather.5.cloned.1.call-start = ((), (), s32[]{:S(2)}) async-start(), calls=%async_computation.8 | async-start | bytes 4456448 | tf_op jit(solution)/shard_map/all_gather | solution.py:42
  34.9 194.8 %reduce-scatter.5.cloned.1.call-start = ((), (), s32[]{:S(2)}) async-start(), calls=%async_computation.9 | async-start | bytes 4456448 | tf_op jit(solution)/shard_map/reduce_scatter | solution.py:46
  79.8 5.9 %copy-start.2 = (bf16[1,4096,512]{2,1,0:T(8,128)(2,1)S(1)}, bf16[1,4096,512]{2,1,0:T(8,128)(2,1)}, u32[]{:S(2)}) copy-start(bf16[1,4096,512]{2,1,0:T(8,128)(2,1)} %param.12) | copy-start | bytes 12582916
  79.8 5.9 %copy-start.5 = (bf16[512,4096]{1,0:T(8,128)(2,1)S(1)}, bf16[512,4096]{1,0:T(8,128)(2,1)}, u32[]{:S(2)}) copy-start(bf16[512,4096]{1,0:T(8,128)(2,1)} %all-gather.3.cloned.1.call-done) | copy-start | bytes 12582916
  138.1 6.6 %copy-start.1 = (bf16[1,4096,512]{2,1,0:T(8,128)(2,1)S(1)}, bf16[1,4096,512]{2,1,0:T(8,128)(2,1)}, u32[]{:S(2)}) copy-start(bf16[1,4096,512]{2,1,0:T(8,128)(2,1)} %param.11) | copy-start | bytes 12582916
  144.7 2.4 copy-start.3
  151.7 159.5 %reduce-scatter.3.cloned.1.call-start = ((), (), s32[]{:S(2)}) async-start(), calls=%async_computation.7 | async-start | bytes 4456448 | tf_op jit(solution)/shard_map/reduce_scatter | solution.py:46
  158.5 165.3 %copy-start.4 = (bf16[128,256]{1,0:T(8,128)(2,1)S(1)}, bf16[128,256]{1,0:T(8,128)(2,1)}, u32[]{:S(2)}) copy-start(bf16[128,256]{1,0:T(8,128)(2,1)} %param.10) | copy-start | bytes 196612
  229.7 81.5 %all-to-all-start.3 = ((bf16[8,64,256]{2,1,0:T(8,128)(2,1)}), bf16[8,64,256]{2,1,0:T(8,128)(2,1)S(1)}, u32[]{:S(2)}, u32[]{:S(2)}) async-start(bf16[8,64,256]{2,1,0:T(8,128)(2,1)} %bitcast.75), calls=%async_computation.5 | async-start | bytes 524288 | tf_op jit(solution)/shard_map/all_to_all | solution.py:49
  311.2 10.9 %all-to-all-start.1 = ((bf16[8,64,256]{2,1,0:T(8,128)(2,1)}), bf16[8,64,256]{2,1,0:T(8,128)(2,1)S(1)}, u32[]{:S(2)}, u32[]{:S(2)}) async-start(bf16[8,64,256]{2,1,0:T(8,128)(2,1)} %bitcast.74), calls=%async_computation.2 | async-start | bytes 524288 | tf_op jit(solution)/shard_map/all_to_all | solution.py:49
  324.6 3.7 %collective-permute-start = (f32[128,2]{0,1:T(2,128)S(1)}, f32[128,2]{0,1:T(2,128)S(1)}, u32[]{:S(2)}, u32[]{:S(2)}) collective-permute-start(f32[128,2]{0,1:T(2,128)S(1)} %pad_maximum_fusion), channel_id=1, source_target_pairs={{0,1},{1,0},{2,3},{3,2},{4,5},{5,4},{6,7},{7,6},{8,9},{9,8},{10,11... | collective-permute-start | bytes 3080 | tf_op jit(solution)/shard_map/ppermute | solution.py:69
  328.3 9.4 %copy-start.6 = (bf16[512,4096]{1,0:T(8,128)(2,1)S(1)}, bf16[512,4096]{1,0:T(8,128)(2,1)}, u32[]{:S(2)}) copy-start(bf16[512,4096]{1,0:T(8,128)(2,1)} %all-gather.3.cloned.1.call-done) | copy-start | bytes 12582916
  328.3 9.1 %collective-permute-start.1 = (f32[128,2]{0,1:T(2,128)S(1)}, f32[128,2]{0,1:T(2,128)S(1)}, u32[]{:S(2)}, u32[]{:S(2)}) collective-permute-start(f32[128,2]{0,1:T(2,128)S(1)} %fusion.40), channel_id=1, source_target_pairs={{0,2},{1,3},{2,0},{3,1},{4,6},{5,7},{6,4},{7,5},{8,10},{9,11},{10,... | collective-permute-start | bytes 3080 | tf_op jit(solution)/shard_map/ppermute | solution.py:69
  337.4 4.8 %collective-permute-start.2 = (f32[128,2]{0,1:T(2,128)S(1)}, f32[128,2]{0,1:T(2,128)S(1)}, u32[]{:S(2)}, u32[]{:S(2)}) collective-permute-start(f32[128,2]{0,1:T(2,128)S(1)} %fusion.54), channel_id=1, source_target_pairs={{0,4},{1,5},{2,6},{3,7},{4,0},{5,1},{6,2},{7,3},{8,12},{9,13},{10,... | collective-permute-start | bytes 3080 | tf_op jit(solution)/shard_map/ppermute | solution.py:69
  342.2 7.2 %collective-permute-start.3 = (f32[128,2]{0,1:T(2,128)S(1)}, f32[128,2]{0,1:T(2,128)S(1)}, u32[]{:S(2)}, u32[]{:S(2)}) collective-permute-start(f32[128,2]{0,1:T(2,128)S(1)} %add.63), channel_id=1, source_target_pairs={{0,8},{1,9},{2,10},{3,11},{4,12},{5,13},{6,14},{7,15},{8,0},{9,1},... | collective-permute-start | bytes 3080 | tf_op jit(solution)/shard_map/ppermute | solution.py:69
Sparse Core Ops, SparseCore 0:
  21.3 58.3 all-gather.2
  81.9 56.2 all-gather.4
  151.8 77.8 reduce-scatter.4
  233.5 77.6 reduce-scatter.2
